TPU v7x, 32 devices: a whole 2x2x4 slice. The times are simulated.
32 devices in a mesh: dp: 4 (over x, core), fsdp: 8 (over z, y).
Axes of the slice: x: 2, y: 2, z: 4, core: 2. Of those that a mesh axis runs over, the one named last changes fastest.
Arguments:
- tokens: bfloat16 [4, 1024, 768], P('dp', 'fsdp'), may hold values from -6 to 6
- ln1_gain: bfloat16 [768], P('fsdp'), may hold values from 0.099609375 to 1.8984375
- ln1_bias: bfloat16 [768], P('fsdp'), may hold values from -1.75 to 1.75
- ln2_gain: bfloat16 [768], P('fsdp'), may hold values from 0.099609375 to 1.8984375
- ln2_bias: bfloat16 [768], P('fsdp'), may hold values from -1.75 to 1.75
- qkv_weight: bfloat16 [768, 2304], P('fsdp'), may hold values from -0.21875 to 0.21875
- qkv_bias: bfloat16 [2304], P('fsdp'), may hold values from -3 to 3
- out_weight: bfloat16 [768, 768], P('fsdp'), may hold values from -1.75 to 1.75
- out_bias: bfloat16 [768], P('fsdp'), may hold values from -3 to 3
- up_weight: bfloat16 [768, 3072], P('fsdp'), may hold values from -0.21875 to 0.21875
- up_bias: bfloat16 [3072], P('fsdp'), may hold values from -3 to 3
- down_weight: bfloat16 [3072, 768], P('fsdp'), may hold values from -0.109375 to 0.109375
- down_bias: bfloat16 [768], P('fsdp'), may hold values from -3 to 3
- cotangent: bfloat16 [4, 1024, 768], P('dp', 'fsdp'), may hold values from -6 to 6
Outputs:
- layer_output: bfloat16 [4, 1024, 768], P('dp', 'fsdp')
- input_grad: float32 [4, 1024, 768], P('dp', 'fsdp')
- grad_ln1_gain: float32 [768], P('fsdp')
- grad_ln1_bias: float32 [768], P('fsdp')
- grad_ln2_gain: float32 [768], P('fsdp')
- grad_ln2_bias: float32 [768], P('fsdp')
- grad_qkv_weight: float32 [768, 2304], P('fsdp')
- grad_qkv_bias: float32 [2304], P('fsdp')
- grad_out_weight: float32 [768, 768], P('fsdp')
- grad_out_bias: float32 [768], P('fsdp')
- grad_up_weight: float32 [768, 3072], P('fsdp')
- grad_up_bias: float32 [3072], P('fsdp')
- grad_down_weight: float32 [3072, 768], P('fsdp')
- grad_down_bias: float32 [768], P('fsdp')
All inputs are finite; a program needn't handle non-finite values.
Results may differ from a plain program's by a relative error of at most 0.018.
Values may be sent and summed in bfloat16 or wider, within the bound.
A program may use at most 128 MiB of HBM per device.

v0:
```python
import math
import jax
import jax.numpy as jnp
from jax import lax
from jax.sharding import PartitionSpec as P

HEADS = 12
HEAD = 64
ROT = 16
epsilon = 1e-05
inv_root_two = 1.0 / math.sqrt(2.0)
inv_root_twopi = 1.0 / math.sqrt(2.0 * math.pi)
bf16 = jnp.bfloat16
f32 = jnp.float32


def rotary(tensor, cosine, sine, direction):
    half = ROT // 2
    first = tensor[..., :half]
    second = tensor[..., half:ROT]
    return jnp.concatenate(
        [
            first * cosine - direction * second * sine,
            second * cosine + direction * first * sine,
            tensor[..., ROT:],
        ],
        axis=-1,
    )


def dot(a, b, dims):
    return lax.dot_general(a, b, ((dims[0], dims[1]), ((), ())), preferred_element_type=f32)


NN = ((1,), (0,))
NT = ((1,), (1,))
TN = ((0,), (0,))


def gather_rows(arrays):
    return [lax.all_gather(a, "fsdp", axis=0, tiled=True) for a in arrays]


def scatter_rows(a):
    return lax.psum_scatter(a, "fsdp", scatter_dimension=0, tiled=True)


def spread_weights(blocks):
    return lax.all_to_all(blocks, "fsdp", 0, 0, tiled=True)


def return_grads(blocks, own):
    summed = lax.psum(blocks, "dp")
    own = lax.psum(own, "dp")
    return (lax.all_to_all(summed, "fsdp", 0, 0, tiled=True), own)


def body(
    tokens,
    ln1_gain,
    ln1_bias,
    ln2_gain,
    ln2_bias,
    qkv_weight,
    qkv_bias,
    out_weight,
    out_bias,
    up_weight,
    up_bias,
    down_weight,
    down_bias,
    cotangent,
):
    rank = lax.axis_index("fsdp")
    F = lax.axis_size("fsdp")
    rows, D = tokens.shape[1:]
    W = D // F
    FFW = down_weight.shape[0]
    NH = max((-(-(g * W % HEAD + W) // HEAD) for g in range(F)))
    WIN = NH * HEAD
    starts = [min(g * W // HEAD, HEADS - NH) * HEAD for g in range(F)]
    start = jnp.minimum(rank * W // HEAD, HEADS - NH) * HEAD
    off = rank * W - start
    S = rows * F
    qkv3 = qkv_weight.reshape(W, 3, D)
    blocks = jnp.stack(
        [
            jnp.concatenate(
                [
                    qkv3[:, 0, s : s + WIN],
                    qkv3[:, 1, s : s + WIN],
                    qkv3[:, 2, s : s + WIN],
                    up_weight[:, g * FFW : (g + 1) * FFW],
                ],
                axis=1,
            )
            for g, s in enumerate(starts)
        ]
    )
    smalls = jnp.concatenate(
        [ln1_gain, ln1_bias, ln2_gain, ln2_bias, out_bias, down_bias, qkv_bias]
    )[None]
    x_low, small_all = gather_rows([tokens[0], smalls])
    wall = spread_weights(blocks).reshape(D, 3 * WIN + FFW)
    w_qkv = wall[:, : 3 * WIN]
    w_up = wall[:, 3 * WIN :]
    up_ring = [(i, (i + 1) % F) for i in range(F)]
    down_ring = [(i, (i - 1) % F) for i in range(F)]
    out_prev = lax.ppermute(out_weight, "fsdp", up_ring)
    out_next = lax.ppermute(out_weight, "fsdp", down_ring)
    (grad_out,) = gather_rows([cotangent[0]])
    out_three = jnp.concatenate([out_prev, out_weight, out_next, jnp.zeros((WIN, D), bf16)], axis=0)
    w_out_win = lax.dynamic_slice_in_dim(out_three, W - off, WIN, 0)
    win_col = jnp.arange(WIN, dtype=jnp.int32)
    mine = (win_col >= off) & (win_col < off + W)
    small_all = small_all.astype(f32)
    gain_one, bias_one, gain_two, bias_two, b_out, b_down = [
        small_all[:, i * W : (i + 1) * W].reshape(D) for i in range(6)
    ]
    b_qkv = small_all[:, 6 * W :].reshape(3, D)
    b_qkv = lax.dynamic_slice_in_dim(b_qkv, start, WIN, 1).reshape(3 * WIN)
    b_up = up_bias.astype(f32)
    x = x_low.astype(f32)
    center = x - jnp.mean(x, axis=-1, keepdims=True)
    inverse = lax.rsqrt(jnp.mean(center * center, axis=-1, keepdims=True) + epsilon)
    normed = center * inverse
    first_low = (normed * gain_one + bias_one).astype(bf16)
    second_low = (normed * gain_two + bias_two).astype(bf16)
    places = jnp.arange(S, dtype=f32)
    half = ROT // 2
    freq = 10000.0 ** (-(jnp.arange(half, dtype=f32) * 2.0) / ROT)
    angle = places[:, None] * freq[None, :]
    cosine = jnp.cos(angle)[:, None, :]
    sine = jnp.sin(angle)[:, None, :]
    proj = dot(first_low, w_qkv, NN) + b_qkv
    queries = (rotary(proj[:, :WIN].reshape(S, NH, HEAD), cosine, sine, 1.0) * 0.125).astype(bf16)
    keys = rotary(proj[:, WIN : 2 * WIN].reshape(S, NH, HEAD), cosine, sine, 1.0).astype(bf16)
    vals = proj[:, 2 * WIN :].astype(bf16).reshape(S, NH, HEAD)
    q_place = jnp.arange(S, dtype=jnp.int32)
    visible = (q_place[None, :] <= q_place[:, None])[None]
    scores = jnp.einsum("qhd,khd->hqk", queries, keys, preferred_element_type=f32)
    masked = jnp.where(visible, scores, -1e30)
    top = jnp.max(masked, axis=-1, keepdims=True)
    lse = top + jnp.log(jnp.sum(jnp.exp(masked - top), axis=-1, keepdims=True))
    probs = jnp.exp(masked - lse)
    probs_low = probs.astype(bf16)
    attended = jnp.einsum("hqk,khd->qhd", probs_low, vals, preferred_element_type=f32)
    att_low = jnp.where(mine, attended.reshape(S, WIN), 0.0).astype(bf16)
    hidden_pre = dot(second_low, w_up, NN) + b_up
    cdf = 0.5 * (1.0 + lax.erf(hidden_pre * inv_root_two))
    hidden_low = (hidden_pre * cdf).astype(bf16)
    part = dot(att_low, w_out_win, NN) + dot(hidden_low, down_weight, NN)
    branch = scatter_rows(part.astype(bf16)).astype(f32)
    grad_hidden = dot(grad_out, down_weight, NT)
    slope = cdf + hidden_pre * jnp.exp(-0.5 * hidden_pre * hidden_pre) * inv_root_twopi
    grad_pre = (grad_hidden * slope).astype(bf16)
    grad_w_down = dot(hidden_low, grad_out, TN)
    grad_w_out_win = dot(att_low, grad_out, TN)
    grad_w_out = lax.dynamic_slice_in_dim(grad_w_out_win, off, W, 0)
    bias_total = jnp.sum(grad_out.astype(f32), axis=0)
    grad_b_up = jnp.sum(grad_pre.astype(f32), axis=0)
    grad_att = dot(grad_out, w_out_win, NT).astype(bf16).reshape(S, NH, HEAD)
    delta = jnp.transpose(jnp.sum(grad_att.astype(f32) * attended, axis=-1))[:, :, None]
    grad_probs = jnp.einsum("qhd,khd->hqk", grad_att, vals, preferred_element_type=f32)
    grad_scores = (probs * (grad_probs - delta)).astype(bf16)
    grad_q = jnp.einsum("hqk,khd->qhd", grad_scores, keys, preferred_element_type=f32)
    grad_k = jnp.einsum("hqk,qhd->khd", grad_scores, queries, preferred_element_type=f32)
    grad_v = jnp.einsum("hqk,qhd->khd", probs_low, grad_att, preferred_element_type=f32)
    grad_proj = jnp.stack(
        [
            rotary(grad_q * 0.125, cosine, sine, -1.0).reshape(S, WIN),
            rotary(grad_k, cosine, sine, -1.0).reshape(S, WIN),
            grad_v.reshape(S, WIN),
        ],
        axis=1,
    )
    grad_proj = jnp.where(mine, grad_proj, 0.0).astype(bf16).reshape(S, 3 * WIN)
    grad_w_qkv = dot(first_low, grad_proj, TN)
    grad_w_up = dot(second_low, grad_pre, TN)
    grad_b_qkv = jnp.sum(grad_proj.astype(f32), axis=0).reshape(3, WIN)
    grad_first = dot(grad_proj, w_qkv, NT)
    grad_second = dot(grad_pre, w_up, NT)
    vectors = [
        jnp.sum(grad_first * normed, axis=0),
        jnp.sum(grad_first, axis=0),
        jnp.sum(grad_second * normed, axis=0),
        jnp.sum(grad_second, axis=0),
    ]
    mixed = grad_first * gain_one + grad_second * gain_two
    b_full = lax.dynamic_update_slice_in_dim(jnp.zeros((3, D), f32), grad_b_qkv, start, 1)
    small_part = jnp.concatenate(
        [v.reshape(F, W) for v in vectors] + [b_full.reshape(F, 3 * W)], axis=1
    )
    mixed_mine = scatter_rows(mixed.astype(bf16)).astype(f32)
    small_mine = scatter_rows(small_part)[0]
    own_small = jnp.concatenate(
        [small_mine, lax.dynamic_slice_in_dim(bias_total, rank * W, W, 0), grad_b_up]
    )
    own_small = lax.psum(own_small, "dp")
    grad_blocks = jnp.concatenate([grad_w_qkv, grad_w_up], axis=1).astype(bf16)
    grad_blocks = grad_blocks.reshape(F, W, 3 * WIN + FFW)
    own = jnp.concatenate([grad_w_out, grad_w_down], axis=0).astype(bf16)
    returned, own = return_grads(grad_blocks, own)
    returned = returned.astype(f32)
    own = own.astype(f32)
    pieces = [
        [
            returned[g, :, i * WIN + g * W - s : i * WIN + g * W - s + W]
            for g, s in enumerate(starts)
        ]
        for i in range(3)
    ]
    out_w_qkv = jnp.concatenate(pieces[0] + pieces[1] + pieces[2], axis=1)
    out_w_up = jnp.concatenate([returned[g, :, 3 * WIN :] for g in range(F)], axis=1)
    here = rank * rows
    x_own = tokens[0].astype(f32)
    c_own = x_own - jnp.mean(x_own, axis=-1, keepdims=True)
    i_own = lax.rsqrt(jnp.mean(c_own * c_own, axis=-1, keepdims=True) + epsilon)
    n_own = c_own * i_own
    layer_output = (x_own + branch + b_out + b_down).astype(bf16)
    input_grad = cotangent[0].astype(f32) + i_own * (
        mixed_mine
        - jnp.mean(mixed_mine, axis=-1, keepdims=True)
        - n_own * jnp.mean(mixed_mine * n_own, axis=-1, keepdims=True)
    )
    g = [own_small[i * W : (i + 1) * W] for i in range(4)]
    bias_mine = own_small[7 * W : 8 * W]
    return (
        layer_output[None],
        input_grad[None],
        g[0],
        g[1],
        g[2],
        g[3],
        out_w_qkv,
        own_small[4 * W : 7 * W],
        own[:W],
        bias_mine,
        out_w_up,
        own_small[8 * W :],
        own[W:],
        bias_mine,
    )


def solution(mesh):
    row = P("fsdp", None)
    vec = P("fsdp")
    act = P("dp", "fsdp", None)
    return jax.shard_map(
        body,
        mesh=mesh,
        in_specs=(act, vec, vec, vec, vec, row, vec, row, vec, row, vec, row, vec, act),
        out_specs=(act, act, vec, vec, vec, vec, row, vec, row, vec, row, vec, row, vec),
        check_vma=False,
    )
```

profile of v0, /device:TPU:0, one launch (start us, length us, event | category | flops | bytes accessed | tf_op | source)
XLA Modules:
  0.0 361.6 jit_solution(6648687961368923165)
XLA Ops:
  7.2 3.0 collective-permute-start
  10.3 3.1 collective-permute-start.1
  22.3 4.2 %all-to-all-start = ((bf16[8,96,768]{2,1,0:T(8,128)(2,1)}), bf16[8,96,768]{2,1,0:T(8,128)(2,1)}, u32[]{:S(2)}, u32[]{:S(2)}) async-start(bf16[8,96,768]{2,1,0:T(8,128)(2,1)} %fusion.81), calls=%async_computation | async-start | bytes 2359296 | tf_op jit(solution)/shard_map/all_to_all | solution.py:49
  29.0 64.6 %all-reduce = bf16[6912]{0:T(1024)(128)(2,1)S(1)} all-reduce(bf16[6912]{0:T(1024)(128)(2,1)S(1)} %dynamic-update-slice), channel_id=3, replica_groups=mesh['dp'=4,'fsdp'=8] {'fsdp'}, use_global_device_ids=true, to_apply=%add | all-reduce | flops 6912 | bytes 27648
  97.8 1.8 convert_reduce_fusion
  100.4 2.2 convolution_add_fusion.1
  109.8 6.8 %all-gather.8.cloned.1.call-done = bf16[1,1024,768]{2,1,0:T(8,128)(2,1)} async-done(((bf16[1,128,768]{2,1,0:T(8,128)(2,1)}), bf16[1,1024,768]{2,1,0:T(8,128)(2,1)}) %all-gather.8.cloned.1.call-update) | async-done | bytes 1572880 | tf_op jit(solution)/shard_map/all_gather | solution.py:41
  116.6 2.2 fusion.36
  118.9 6.5 %fusion.41 = (f32[1024,2]{0,1:T(2,128)S(1)}, bf16[2,64,1024]{2,1,0:T(8,128)(2,1)}) fusion(bf16[128,1024]{1,0:T(8,128)(2,1)S(1)} %fusion.36, bf16[1024,2,64]{0,2,1:T(8,128)(2,1)S(1)} %bitcast.330, f32[2,1024,1024]{1,2,0:T(8,128)} %copy-done.4, f32[2,1024]{1,0:T(2,128)S(1)} %copy-done.23, pred[1024,1024]{0,1:T(8,128)(4,1)S(1)} %iota_compare_fusion), kind=kOutput, calls=%fused_computation.73 | convolution fusion | flops 275249152 | bytes 10240000 | tf_op jit(solution)/shard_map/hqk,khd->qhd/dot_general | solution.py:147
  125.3 3.3 multiply_convert_fusion
  131.0 2.4 fusion.83
  136.0 2.3 multiply_convert_fusion.1
  139.6 2.1 fusion.42
  141.7 1.8 convolution_convert_fusion
  144.2 4.6 %fusion.99 = (f32[768]{0:T(1024)S(1)}, f32[768]{0:T(1024)S(1)}, bf16[1024,768]{1,0:T(8,128)(2,1)}, f32[768]{0:T(1024)S(1)}, f32[768]{0:T(1024)S(1)}, /*index=5*/bf16[768,1024]{0,1:T(8,128)(2,1)}) fusion(f32[1024,768]{1,0:T(8,128)S(1)} %fusion.42, f32[1024]{0:T(1024)S(1)} %add_rsqrt_fusion, f32[1024]{0:T(1024)S(1)} %broadcast_multiply_fusion.1, ...), kind=kOutput, calls=%fused_computation.216 | convolution fusion | flops 616559616 | bytes 9270272 | tf_op jit(solution)/shard_map/dot_general | solution.py:32
  151.7 2.2 convolution_convert_fusion.1
  158.5 46.5 %all-reduce.5.cloned.1.call-done = (bf16[8,96,768]{2,1,0:T(8,128)(2,1)}, bf16[480,768]{1,0:T(8,128)(2,1)}) async-done(((bf16[8,96,768]{2,1,0:T(8,128)(2,1)}, bf16[480,768]{1,0:T(8,128)(2,1)}), (bf16[8,96,768]{2,1,0:T(8,128)(2,1)}, bf16[480,768]{1,0:T(8,128)(2,1)})) %all-reduce.5.cloned.1.call-update) | async-done | bytes 1916944 | tf_op jit(solution)/shard_map/psum | solution.py:53
  205.0 5.5 %all-to-all-start.1 = ((bf16[8,96,768]{2,1,0:T(8,128)(2,1)}), bf16[8,96,768]{2,1,0:T(8,128)(2,1)}, u32[]{:S(2)}, u32[]{:S(2)}) async-start(bf16[8,96,768]{2,1,0:T(8,128)(2,1)} %get-tuple-element.20), calls=%async_computation.3 | async-start | bytes 2359296 | tf_op jit(solution)/shard_map/all_to_all | solution.py:55
  212.1 63.2 %all-reduce.1 = f32[8,672]{1,0:T(8,128)S(1)} all-reduce(f32[8,672]{1,0:T(8,128)S(1)} %concatenate.80), channel_id=7, replica_groups=mesh['dp'=4,'fsdp'=8] {'fsdp'}, use_global_device_ids=true, to_apply=%region_16.17.clone | all-reduce | flops 5376 | bytes 43008
  276.0 6.1 %psum.21 = f32[1152]{0:T(1024)S(1)} all-reduce(f32[1152]{0:T(1024)S(1)} %concatenate.81), channel_id=1, replica_groups=mesh['dp'=4,'fsdp'=8] {'dp'}, use_global_device_ids=true, to_apply=%region_19.20 | all-reduce | flops 1152 | bytes 9216 | tf_op jit(solution)/shard_map/psum | solution.py:199
  284.3 2.7 add_convert_fusion.1
  292.5 2.3 concatenate.84
  301.4 51.2 %reduce-scatter.3.cloned.1.call-done = bf16[128,768]{1,0:T(8,128)(2,1)} async-done(((bf16[1024,768]{1,0:T(8,128)(2,1)}), bf16[128,768]{1,0:T(8,128)(2,1)}) %reduce-scatter.3.cloned.1.call-update) | async-done | bytes 196624 | tf_op jit(solution)/shard_map/reduce_scatter | solution.py:45
  352.6 2.0 fusion.56
  (217 shorter events, 53.6 us)
Async XLA Ops:
  7.2 131.1 %copy-start = (bf16[384,768]{1,0:T(8,128)(2,1)S(1)}, bf16[384,768]{1,0:T(8,128)(2,1)}, u32[]{:S(2)}) copy-start(bf16[384,768]{1,0:T(8,128)(2,1)} %param.25) | copy-start | bytes 1769476
  7.2 90.6 %all-gather.6.cloned.1.call-start = ((), (), s32[]{:S(2)}) async-start(), calls=%async_computation.6 | async-start | bytes 1769472 | tf_op jit(solution)/shard_map/all_gather | solution.py:41
  7.2 102.6 %collective-permute-start = (bf16[96,768]{1,0:T(8,128)(2,1)}, bf16[96,768]{1,0:T(8,128)(2,1)}, u32[]{:S(2)}, u32[]{:S(2)}) collective-permute-start(bf16[96,768]{1,0:T(8,128)(2,1)} %param.21), channel_id=1, source_target_pairs={{0,1},{1,2},{2,3},{3,4},{4,5},{5,6},{6,7},{7,0},{8,9},{9,10},{10,1... | collective-permute-start | bytes 442376 | tf_op jit(solution)/shard_map/ppermute | solution.py:109
  10.3 99.5 %collective-permute-start.1 = (bf16[96,768]{1,0:T(8,128)(2,1)}, bf16[96,768]{1,0:T(8,128)(2,1)}, u32[]{:S(2)}, u32[]{:S(2)}) collective-permute-start(bf16[96,768]{1,0:T(8,128)(2,1)} %param.21), channel_id=1, source_target_pairs={{0,7},{1,0},{2,1},{3,2},{4,3},{5,4},{6,5},{7,6},{8,15},{9,8},{10,9... | collective-permute-start | bytes 442376 | tf_op jit(solution)/shard_map/ppermute | solution.py:110
  21.5 7.1 %copy-start.33 = (bf16[288]{0:T(512)(128)(2,1)S(1)}, bf16[288]{0:T(512)(128)(2,1)}, u32[]{:S(2)}) copy-start(bf16[288]{0:T(512)(128)(2,1)} %param.20) | copy-start | bytes 1732
  21.5 7.1 %copy-start.36 = (bf16[96]{0:T(256)(128)(2,1)S(1)}, bf16[96]{0:T(256)(128)(2,1)}, u32[]{:S(2)}) copy-start(bf16[96]{0:T(256)(128)(2,1)} %param.15) | copy-start | bytes 580
  21.5 7.1 %copy-start.37 = (bf16[96]{0:T(256)(128)(2,1)S(1)}, bf16[96]{0:T(256)(128)(2,1)}, u32[]{:S(2)}) copy-start(bf16[96]{0:T(256)(128)(2,1)} %param.16) | copy-start | bytes 580
  21.5 7.1 %copy-start.38 = (bf16[96]{0:T(256)(128)(2,1)S(1)}, bf16[96]{0:T(256)(128)(2,1)}, u32[]{:S(2)}) copy-start(bf16[96]{0:T(256)(128)(2,1)} %param.17) | copy-start | bytes 580
  21.5 7.1 %copy-start.39 = (bf16[96]{0:T(256)(128)(2,1)S(1)}, bf16[96]{0:T(256)(128)(2,1)}, u32[]{:S(2)}) copy-start(bf16[96]{0:T(256)(128)(2,1)} %param.18) | copy-start | bytes 580
  21.5 7.1 %copy-start.40 = (bf16[96]{0:T(256)(128)(2,1)S(1)}, bf16[96]{0:T(256)(128)(2,1)}, u32[]{:S(2)}) copy-start(bf16[96]{0:T(256)(128)(2,1)} %param.22) | copy-start | bytes 580
  21.5 7.1 %copy-start.41 = (bf16[96]{0:T(256)(128)(2,1)S(1)}, bf16[96]{0:T(256)(128)(2,1)}, u32[]{:S(2)}) copy-start(bf16[96]{0:T(256)(128)(2,1)} %param.26) | copy-start | bytes 580
  21.6 73.3 %copy-start.32 = (bf16[384]{0:T(512)(128)(2,1)S(1)}, bf16[384]{0:T(512)(128)(2,1)}, u32[]{:S(2)}) copy-start(bf16[384]{0:T(512)(128)(2,1)} %param.24) | copy-start | bytes 2308
  22.3 78.1 %all-to-all-start = ((bf16[8,96,768]{2,1,0:T(8,128)(2,1)}), bf16[8,96,768]{2,1,0:T(8,128)(2,1)}, u32[]{:S(2)}, u32[]{:S(2)}) async-start(bf16[8,96,768]{2,1,0:T(8,128)(2,1)} %fusion.81), calls=%async_computation | async-start | bytes 2359296 | tf_op jit(solution)/shard_map/all_to_all | solution.py:49
  26.5 90.1 %all-gather.8.cloned.1.call-start = ((), (), s32[]{:S(2)}) async-start(), calls=%async_computation.7 | async-start | bytes 1769472 | tf_op jit(solution)/shard_map/all_gather | solution.py:41
  27.3 177.7 %all-reduce.5.cloned.1.call-start = ((), (), s32[]{:S(2)}) async-start(), calls=%async_computation.8 | async-start | bytes 3833856 | tf_op jit(solution)/shard_map/psum | solution.py:53
  118.8 6.5 %copy-start.5 = (f32[2,1024,1024]{1,2,0:T(8,128)S(1)}, f32[2,1024,1024]{1,2,0:T(8,128)}, u32[]{:S(2)}) copy-start(f32[2,1024,1024]{1,2,0:T(8,128)} %copy-done.4) | copy-start | bytes 25165828
  157.9 142.4 %reduce-scatter.5.cloned.1.call-start = ((), (), s32[]{:S(2)}) async-start(), calls=%async_computation.5 | async-start | bytes 1769472 | tf_op jit(solution)/shard_map/reduce_scatter | solution.py:45
  158.4 52.1 %copy-start.22 = (f32[8,96]{1,0:T(8,128)S(1)}, f32[8,96]{1,0:T(8,128)}, u32[]{:S(2)}) copy-start(f32[8,96]{1,0:T(8,128)} %get-tuple-element.100) | copy-start | bytes 9220
  158.4 52.2 %copy-start.21 = (f32[8,96]{1,0:T(8,128)S(1)}, f32[8,96]{1,0:T(8,128)}, u32[]{:S(2)}) copy-start(f32[8,96]{1,0:T(8,128)} %get-tuple-element.101) | copy-start | bytes 9220
  158.5 52.3 %copy-start.6 = (bf16[1,128,768]{2,1,0:T(8,128)(2,1)S(1)}, bf16[1,128,768]{2,1,0:T(8,128)(2,1)}, u32[]{:S(2)}) copy-start(bf16[1,128,768]{2,1,0:T(8,128)(2,1)} %param.14) | copy-start | bytes 589828
  205.0 84.9 %all-to-all-start.1 = ((bf16[8,96,768]{2,1,0:T(8,128)(2,1)}), bf16[8,96,768]{2,1,0:T(8,128)(2,1)}, u32[]{:S(2)}, u32[]{:S(2)}) async-start(bf16[8,96,768]{2,1,0:T(8,128)(2,1)} %get-tuple-element.20), calls=%async_computation.3 | async-start | bytes 2359296 | tf_op jit(solution)/shard_map/all_to_all | solution.py:55
  210.5 142.1 %reduce-scatter.3.cloned.1.call-start = ((), (), s32[]{:S(2)}) async-start(), calls=%async_computation.4 | async-start | bytes 1769472 | tf_op jit(solution)/shard_map/reduce_scatter | solution.py:45
  294.9 57.7 %copy-start.10 = (bf16[1,128,768]{2,1,0:T(8,128)(2,1)S(1)}, bf16[1,128,768]{2,1,0:T(8,128)(2,1)}, u32[]{:S(2)}) copy-start(bf16[1,128,768]{2,1,0:T(8,128)(2,1)} %param.27) | copy-start | bytes 589828
  296.9 57.7 %copy-start.42 = (f32[96]{0:T(128)S(1)}, f32[96]{0:T(128)}, u32[]{:S(2)}) copy-start(f32[96]{0:T(128)} %get-tuple-element.175) | copy-start | bytes 1156
  (28 other events, 63.2 us)
Sparse Core Ops, SparseCore 0:
  13.5 57.5 all-gather.5
  73.3 43.2 all-gather.7
  158.0 46.9 all-reduce.4
  208.3 76.4 reduce-scatter.4
  288.0 64.5 reduce-scatter.2
where the time goes:
time: 363 us; the launch traced here: 362 us
  blocking collectives  134 us (37%)
  waiting for transfers between devices  106 us (29%)
  matrix products  39.7 us (11%)
  local copies, waits for them, and re-layouts  28.3 us (8%)
  other arithmetic  22.5 us (6%)
  starting transfers between devices  16.1 us (4%)
  between operations  15.3 us (4%)
    unnamed x2, blocking collectives  128 us
    reduce_scatter x2, waiting for transfers between devices, scatter_rows(): return lax.psum_scatter(a, 'fsdp', scatter_dimension=0, tiled=True)  51.2 us
    psum x1, waiting for transfers between devices, return_grads(): summed = lax.psum(blocks, 'dp')  46.5 us
    dot_general x12, matrix products, dot(): lax.dot_general(a, b, ((dims[0], dims[1]), ((), ())), preferred_element_t...  23.6 us
    unnamed x110, local copies, waits for them, and re-layouts  10.9 us
  transfers between devices with their start and end apart: 9, of which 3 were waited for; matrix products, arithmetic and copies ran while one was open for 12% of the time, Pallas kernels for 0%

commit v1 on v0

--- a/solution.py
+++ b/solution.py
@@ -50,7 +50,17 @@
 
 
 def return_grads(blocks, own):
-    summed = lax.psum(blocks, "dp")
+
+    def sector_detail(local_x):
+        n_slots = lax.psum(1, "dp")
+        long_array = local_x
+        for h in [w for w in (1, 2, 4, 8, 16) if w < n_slots]:
+            long_array = long_array + lax.ppermute(
+                long_array, "dp", tuple(((i0, i0 ^ h) for i0 in range(n_slots)))
+            )
+        return long_array
+
+    summed = sector_detail(blocks)
     own = lax.psum(own, "dp")
     return (lax.all_to_all(summed, "fsdp", 0, 0, tiled=True), own)
 

time: 363 us -> 344 us (0.948)
  blocking collectives: 134 us -> 115 us
  waiting for transfers between devices: 106 us -> 92.8 us
  local copies, waits for them, and re-layouts: 28.3 us -> 33.8 us
  other arithmetic: 22.5 us -> 27.7 us
    psum x1, waiting for transfers between devices: 46.5 us -> 0.02 us  [return_grads(): own = lax.psum(own, 'dp')]
    ppermute x0 -> x2, waiting for transfers between devices: none -> 31.4 us  [sector_detail(): lax.ppermute(long_array, 'dp', tuple(((i0, i0 ^ h) for i0 in range(n_slot...]
    unnamed x2, blocking collectives: 128 us -> 110 us
    reshape x4, local copies, waits for them, and re-layouts: 0.28 us -> 5.4 us  [body(): v.reshape(F, W)]
    unnamed x110 -> x134, local copies, waits for them, and re-layouts: 10.9 us -> 5.81 us
  transfers between devices with their start and end apart: 9 -> 11, of which waited for: 3 -> 3; matrix products, arithmetic and copies ran while one was open for 12% -> 19% of each run, Pallas kernels for 0% -> 0%
where the time goes in v1:
time: 344 us; the launch traced here: 343 us
  blocking collectives  115 us (33%)
  waiting for transfers between devices  92.8 us (27%)
  matrix products  41.3 us (12%)
  local copies, waits for them, and re-layouts  33.8 us (10%)
  other arithmetic  27.7 us (8%)
  starting transfers between devices  16.7 us (5%)
  between operations  15.4 us (4%)
    unnamed x2, blocking collectives  110 us
    reduce_scatter x2, waiting for transfers between devices, scatter_rows(): return lax.psum_scatter(a, 'fsdp', scatter_dimension=0, tiled=True)  54 us
    ppermute x2, waiting for transfers between devices, sector_detail(): lax.ppermute(long_array, 'dp', tuple(((i0, i0 ^ h) for i0 in range(n_slot...  31.4 us
    dot_general x12, matrix products, dot(): lax.dot_general(a, b, ((dims[0], dims[1]), ((), ())), preferred_element_t...  25.2 us
  transfers between devices with their start and end apart: 11, of which 3 were waited for; matrix products, arithmetic and copies ran while one was open for 19% of the time, Pallas kernels for 0%

profile of v1, /device:TPU:0, one launch (start us, length us, event | category | flops | bytes accessed | tf_op | source)
XLA Modules:
  0.0 343.1 jit_solution(17634597714265639272)
XLA Ops:
  7.2 3.0 collective-permute-start
  10.3 3.1 collective-permute-start.1
  22.3 4.3 %all-to-all-start = ((bf16[8,96,768]{2,1,0:T(8,128)(2,1)}), bf16[8,96,768]{2,1,0:T(8,128)(2,1)}, u32[]{:S(2)}, u32[]{:S(2)}) async-start(bf16[8,96,768]{2,1,0:T(8,128)(2,1)} %fusion.81), calls=%async_computation | async-start | bytes 2359296 | tf_op jit(solution)/shard_map/all_to_all | solution.py:49
  29.0 64.7 %all-reduce = bf16[6912]{0:T(1024)(128)(2,1)S(1)} all-reduce(bf16[6912]{0:T(1024)(128)(2,1)S(1)} %dynamic-update-slice), channel_id=3, replica_groups=mesh['dp'=4,'fsdp'=8] {'fsdp'}, use_global_device_ids=true, to_apply=%add | all-reduce | flops 6912 | bytes 27648
  97.9 1.8 convert_reduce_fusion
  100.4 2.2 convolution_add_fusion.1
  109.8 6.7 %all-gather.8.cloned.1.call-done = bf16[1,1024,768]{2,1,0:T(8,128)(2,1)} async-done(((bf16[1,128,768]{2,1,0:T(8,128)(2,1)}), bf16[1,1024,768]{2,1,0:T(8,128)(2,1)}) %all-gather.8.cloned.1.call-update) | async-done | bytes 1572880 | tf_op jit(solution)/shard_map/all_gather | solution.py:41
  116.5 2.2 fusion.36
  118.7 5.8 %fusion.41 = (f32[1024,2]{0,1:T(2,128)S(1)}, bf16[2,64,1024]{2,1,0:T(8,128)(2,1)S(1)}) fusion(bf16[128,1024]{1,0:T(8,128)(2,1)S(1)} %fusion.36, bf16[1024,2,64]{0,2,1:T(8,128)(2,1)S(1)} %bitcast.331, f32[2,1024,1024]{1,2,0:T(8,128)} %copy-done.4, f32[2,1024]{1,0:T(2,128)S(1)} %copy-done.33, pred[1024,1024]{0,1:T(8,128)(4,1)S(1)} %iota_compare_fusion), kind=kOutput, calls=%fused_computation.73 | convolution fusion | flops 275249152 | bytes 10240000 | tf_op jit(solution)/shard_map/hqk,khd->qhd/dot_general | solution.py:157
  124.5 3.3 multiply_convert_fusion
  130.2 3.1 fusion.83
  136.1 2.7 multiply_convert_fusion.1
  138.8 1.9 convert_reduce_fusion.2
  140.8 4.0 %fusion.42 = f32[1024,768]{1,0:T(8,128)} fusion(bf16[1024,384]{1,0:T(8,128)(2,1)S(1)} %get-tuple-element.121, bf16[768,768]{1,0:T(8,128)(2,1)} %bitcast.11), kind=kOutput, calls=%fused_computation.74 | convolution fusion | flops 603979776 | bytes 4521984 | tf_op jit(solution)/shard_map/dot_general | solution.py:32
  151.9 5.3 %fusion.100 = (f32[768]{0:T(1024)}, f32[768]{0:T(1024)}, bf16[1024,768]{1,0:T(8,128)(2,1)}, f32[768]{0:T(1024)}, f32[768]{0:T(1024)}, /*index=5*/bf16[768,1024]{0,1:T(8,128)(2,1)}) fusion(f32[1024,768]{1,0:T(8,128)S(1)} %copy-done.7, f32[1024]{0:T(1024)S(1)} %add_rsqrt_fusion, f32[1024]{0:T(1024)S(1)} %broadcast_multiply_fusion.1, ...), kind=kOutput, calls=%fused_computation.217 | convolution fusion | flops 616559616 | bytes 9270272 | tf_op jit(solution)/shard_map/dot_general | solution.py:32
  157.3 3.0 copy.54
  166.3 2.7 add_convert_fusion.1
  172.0 31.4 %collective-permute-done.3 = bf16[8,96,768]{2,1,0:T(8,128)(2,1)S(1)} collective-permute-done((bf16[8,96,768]{2,1,0:T(8,128)(2,1)S(1)}, bf16[8,96,768]{2,1,0:T(8,128)(2,1)S(1)}, u32[]{:S(2)}, u32[]{:S(2)}) %collective-permute-start.3) | collective-permute-done | bytes 1179680 | tf_op jit(solution)/shard_map/ppermute | solution.py:58
  204.7 4.6 %all-to-all-start.1 = ((bf16[8,96,768]{2,1,0:T(8,128)(2,1)}), bf16[8,96,768]{2,1,0:T(8,128)(2,1)S(1)}, u32[]{:S(2)}, u32[]{:S(2)}) async-start(bf16[8,96,768]{2,1,0:T(8,128)(2,1)} %add.193), calls=%async_computation.3 | async-start | bytes 2359296 | tf_op jit(solution)/shard_map/all_to_all | solution.py:65
  219.0 45.1 %all-reduce.1 = f32[8,672]{1,0:T(8,128)S(1)} all-reduce(f32[8,672]{1,0:T(8,128)S(1)} %concatenate.80), channel_id=7, replica_groups=mesh['dp'=4,'fsdp'=8] {'fsdp'}, use_global_device_ids=true, to_apply=%region_16.17.clone | all-reduce | flops 5376 | bytes 43008
  265.5 5.7 %psum.14 = f32[1152]{0:T(1024)S(1)} all-reduce(f32[1152]{0:T(1024)S(1)} %concatenate.81), channel_id=1, replica_groups=mesh['dp'=4,'fsdp'=8] {'dp'}, use_global_device_ids=true, to_apply=%region_19.20 | all-reduce | flops 1152 | bytes 9216 | tf_op jit(solution)/shard_map/psum | solution.py:209
  273.0 2.2 slice.478
  278.1 54.0 %reduce-scatter.3.cloned.1.call-done = bf16[128,768]{1,0:T(8,128)(2,1)} async-done(((bf16[1024,768]{1,0:T(8,128)(2,1)}), bf16[128,768]{1,0:T(8,128)(2,1)}) %reduce-scatter.3.cloned.1.call-update) | async-done | bytes 196624 | tf_op jit(solution)/shard_map/reduce_scatter | solution.py:45
  332.1 2.0 fusion.56
  (247 shorter events, 63.0 us)
Async XLA Ops:
  7.2 131.6 %copy-start = (bf16[384,768]{1,0:T(8,128)(2,1)S(1)}, bf16[384,768]{1,0:T(8,128)(2,1)}, u32[]{:S(2)}) copy-start(bf16[384,768]{1,0:T(8,128)(2,1)} %param.25) | copy-start | bytes 1769476
  7.2 90.7 %all-gather.6.cloned.1.call-start = ((), (), s32[]{:S(2)}) async-start(), calls=%async_computation.7 | async-start | bytes 1769472 | tf_op jit(solution)/shard_map/all_gather | solution.py:41
  7.2 102.5 %collective-permute-start = (bf16[96,768]{1,0:T(8,128)(2,1)}, bf16[96,768]{1,0:T(8,128)(2,1)}, u32[]{:S(2)}, u32[]{:S(2)}) collective-permute-start(bf16[96,768]{1,0:T(8,128)(2,1)} %param.21), channel_id=1, source_target_pairs={{0,1},{1,2},{2,3},{3,4},{4,5},{5,6},{6,7},{7,0},{8,9},{9,10},{10,1... | collective-permute-start | bytes 442376 | tf_op jit(solution)/shard_map/ppermute | solution.py:119
  10.3 99.5 %collective-permute-start.1 = (bf16[96,768]{1,0:T(8,128)(2,1)}, bf16[96,768]{1,0:T(8,128)(2,1)}, u32[]{:S(2)}, u32[]{:S(2)}) collective-permute-start(bf16[96,768]{1,0:T(8,128)(2,1)} %param.21), channel_id=1, source_target_pairs={{0,7},{1,0},{2,1},{3,2},{4,3},{5,4},{6,5},{7,6},{8,15},{9,8},{10,9... | collective-permute-start | bytes 442376 | tf_op jit(solution)/shard_map/ppermute | solution.py:120
  21.5 7.1 %copy-start.49 = (bf16[96]{0:T(256)(128)(2,1)S(1)}, bf16[96]{0:T(256)(128)(2,1)}, u32[]{:S(2)}) copy-start(bf16[96]{0:T(256)(128)(2,1)} %param.16) | copy-start | bytes 580
  21.5 7.1 %copy-start.50 = (bf16[96]{0:T(256)(128)(2,1)S(1)}, bf16[96]{0:T(256)(128)(2,1)}, u32[]{:S(2)}) copy-start(bf16[96]{0:T(256)(128)(2,1)} %param.17) | copy-start | bytes 580
  21.5 7.1 %copy-start.51 = (bf16[96]{0:T(256)(128)(2,1)S(1)}, bf16[96]{0:T(256)(128)(2,1)}, u32[]{:S(2)}) copy-start(bf16[96]{0:T(256)(128)(2,1)} %param.18) | copy-start | bytes 580
  21.5 7.1 %copy-start.52 = (bf16[96]{0:T(256)(128)(2,1)S(1)}, bf16[96]{0:T(256)(128)(2,1)}, u32[]{:S(2)}) copy-start(bf16[96]{0:T(256)(128)(2,1)} %param.22) | copy-start | bytes 580
  21.5 7.1 %copy-start.53 = (bf16[96]{0:T(256)(128)(2,1)S(1)}, bf16[96]{0:T(256)(128)(2,1)}, u32[]{:S(2)}) copy-start(bf16[96]{0:T(256)(128)(2,1)} %param.26) | copy-start | bytes 580
  21.6 73.3 %copy-start.45 = (bf16[384]{0:T(512)(128)(2,1)S(1)}, bf16[384]{0:T(512)(128)(2,1)}, u32[]{:S(2)}) copy-start(bf16[384]{0:T(512)(128)(2,1)} %param.24) | copy-start | bytes 2308
  22.3 78.1 %all-to-all-start = ((bf16[8,96,768]{2,1,0:T(8,128)(2,1)}), bf16[8,96,768]{2,1,0:T(8,128)(2,1)}, u32[]{:S(2)}, u32[]{:S(2)}) async-start(bf16[8,96,768]{2,1,0:T(8,128)(2,1)} %fusion.81), calls=%async_computation | async-start | bytes 2359296 | tf_op jit(solution)/shard_map/all_to_all | solution.py:49
  26.5 89.9 %all-gather.8.cloned.1.call-start = ((), (), s32[]{:S(2)}) async-start(), calls=%async_computation.8 | async-start | bytes 1769472 | tf_op jit(solution)/shard_map/all_gather | solution.py:41
  27.3 245.7 %all-reduce.4.cloned.1.call-start = ((), (), s32[]{:S(2)}) async-start(), calls=%async_computation.6 | async-start | bytes 1474560 | tf_op jit(solution)/shard_map/psum | solution.py:64
  147.1 129.8 %reduce-scatter.5.cloned.1.call-start = ((), (), s32[]{:S(2)}) async-start(), calls=%async_computation.5 | async-start | bytes 1769472 | tf_op jit(solution)/shard_map/reduce_scatter | solution.py:45
  157.2 174.9 %reduce-scatter.3.cloned.1.call-start = ((), (), s32[]{:S(2)}) async-start(), calls=%async_computation.4 | async-start | bytes 1769472 | tf_op jit(solution)/shard_map/reduce_scatter | solution.py:45
  165.3 3.7 %collective-permute-start.2 = (bf16[8,96,768]{2,1,0:T(8,128)(2,1)}, bf16[8,96,768]{2,1,0:T(8,128)(2,1)}, u32[]{:S(2)}, u32[]{:S(2)}) collective-permute-start(bf16[8,96,768]{2,1,0:T(8,128)(2,1)} %pad_maximum_fusion.1), channel_id=1, source_target_pairs={{0,8},{8,0},{16,24},{24,16},{1,9},{9,1},{17,25},{25,17},{2,10},{10... | collective-permute-start | bytes 3538952 | tf_op jit(solution)/shard_map/ppermute | solution.py:58
  170.6 32.8 %collective-permute-start.3 = (bf16[8,96,768]{2,1,0:T(8,128)(2,1)S(1)}, bf16[8,96,768]{2,1,0:T(8,128)(2,1)S(1)}, u32[]{:S(2)}, u32[]{:S(2)}) collective-permute-start(bf16[8,96,768]{2,1,0:T(8,128)(2,1)S(1)} %fusion.95), channel_id=1, source_target_pairs={{0,16},{8,24},{16,0},{24,8},{1,17},{9,25},{17,1},{25,9},{2,18},{10... | collective-permute-start | bytes 3538952 | tf_op jit(solution)/shard_map/ppermute | solution.py:58
  204.7 13.1 %copy-start.3 = (bf16[1,1024,768]{2,1,0:T(8,128)(2,1)S(1)}, bf16[1,1024,768]{2,1,0:T(8,128)(2,1)}, u32[]{:S(2)}) copy-start(bf16[1,1024,768]{2,1,0:T(8,128)(2,1)} %all-gather.8.cloned.1.call-done) | copy-start | bytes 4718596
  204.7 129.3 %all-to-all-start.1 = ((bf16[8,96,768]{2,1,0:T(8,128)(2,1)}), bf16[8,96,768]{2,1,0:T(8,128)(2,1)S(1)}, u32[]{:S(2)}, u32[]{:S(2)}) async-start(bf16[8,96,768]{2,1,0:T(8,128)(2,1)} %add.193), calls=%async_computation.3 | async-start | bytes 2359296 | tf_op jit(solution)/shard_map/all_to_all | solution.py:65
  218.1 58.8 %copy-start.35 = (f32[128]{0:T(128)S(1)}, f32[128]{0:T(128)}, u32[]{:S(2)}) copy-start(f32[128]{0:T(128)} %copy-done.34) | copy-start | bytes 1540
  218.1 58.8 %copy-start.42 = (f32[128]{0:T(128)S(1)}, f32[128]{0:T(128)}, u32[]{:S(2)}) copy-start(f32[128]{0:T(128)} %add_rsqrt_fusion.1) | copy-start | bytes 1540
  273.0 63.1 %copy-start.54 = (f32[96]{0:T(128)}, f32[96]{0:T(128)S(1)}, u32[]{:S(2)}) copy-start(f32[96]{0:T(128)S(1)} %get-tuple-element.173) | copy-start | bytes 1156
  273.0 59.1 %copy-start.16 = (bf16[1,128,768]{2,1,0:T(8,128)(2,1)S(1)}, bf16[1,128,768]{2,1,0:T(8,128)(2,1)}, u32[]{:S(2)}) copy-start(bf16[1,128,768]{2,1,0:T(8,128)(2,1)} %param.27) | copy-start | bytes 589828
  273.0 59.1 %copy-start.30 = (f32[768]{0:T(1024)S(1)}, f32[768]{0:T(1024)}, u32[]{:S(2)}) copy-start(f32[768]{0:T(1024)} %add.181) | copy-start | bytes 9220
  (42 other events, 132.8 us)
Sparse Core Ops, SparseCore 0:
  13.5 57.5 all-gather.5
  73.3 43.1 all-gather.7
  147.2 35.7 all-reduce.3
  186.3 77.8 reduce-scatter.4
  267.4 64.5 reduce-scatter.2
